TPU v7x, 32 devices: a whole 2x2x4 slice. The times are simulated.
32 devices in a mesh: dp: 8 (over z, y), tensor: 4 (over x, core).
Axes of the slice: x: 2, y: 2, z: 4, core: 2. Of those that a mesh axis runs over, the one named last changes fastest.
Arguments:
- tokens: bfloat16 [8192, 1024], P(('dp', 'tensor')), may hold values from -16 to 16
- cotangent: bfloat16 [8192, 1024], P(('dp', 'tensor')), may hold values from -16 to 16
- gain_attn: float32 [1024], replicated, may hold values from 0.1 to 1.9
- bias_attn: float32 [1024], replicated, may hold values from -1.75 to 1.75
- gain_mlp: float32 [1024], replicated, may hold values from 0.1 to 1.9
- bias_mlp: float32 [1024], replicated, may hold values from -1.75 to 1.75
- qkv_weight: bfloat16 [1024, 3072], P(None, 'tensor'), may hold values from -0.1875 to 0.1875
- qkv_bias: float32 [3072], P('tensor'), may hold values from -1.75 to 1.75
- out_weight: bfloat16 [1024, 1024], P('tensor'), may hold values from -2.5 to 2.5
- out_bias: float32 [1024], replicated, may hold values from -1.75 to 1.75
- up_weight: bfloat16 [1024, 4096], P(None, 'tensor'), may hold values from -0.1875 to 0.1875
- up_bias: float32 [4096], P('tensor'), may hold values from -1.75 to 1.75
- down_weight: bfloat16 [4096, 1024], P('tensor'), may hold values from -0.09375 to 0.09375
- down_bias: float32 [1024], replicated, may hold values from -1.75 to 1.75
Outputs:
- mixed: bfloat16 [8192, 1024], P(('dp', 'tensor'))
- input_grad: float32 [8192, 1024], P(('dp', 'tensor'))
- gain_attn_grad: float32 [1024], replicated
- bias_attn_grad: float32 [1024], replicated
- gain_mlp_grad: float32 [1024], replicated
- bias_mlp_grad: float32 [1024], replicated
- qkv_weight_grad: float32 [1024, 3072], P(None, 'tensor')
- qkv_bias_grad: float32 [3072], P('tensor')
- out_weight_grad: float32 [1024, 1024], P('tensor')
- out_bias_grad: float32 [1024], replicated
- up_weight_grad: float32 [1024, 4096], P(None, 'tensor')
- up_bias_grad: float32 [4096], P('tensor')
- down_weight_grad: float32 [4096, 1024], P('tensor')
- down_bias_grad: float32 [1024], replicated
- statistics: float32 [3], replicated
All inputs are finite; a program needn't handle non-finite values.
Results may differ from a plain program's by a relative error of at most 0.012.
The roundings to bfloat16 on the way count: a program that leaves them out, or rounds other values in their place, can miss the bound.
Values may be sent and summed in bfloat16 or wider, within the bound.
A program may use at most 192 MiB of HBM per device.

v0:
```python
import math
import jax
import jax.numpy as jnp
from jax import lax
from jax.sharding import PartitionSpec as P

HD = 64
ROT = 16
epsilon = 1e-05


def angle_tables(seq_len):
    positions = jnp.arange(seq_len, dtype=jnp.float32)
    inverse = 10000.0 ** (-(jnp.arange(ROT // 2, dtype=jnp.float32) * 2.0 / ROT))
    angles = positions[:, None] * inverse[None, :]
    cosine = jnp.concatenate([jnp.cos(angles), jnp.cos(angles)], axis=-1)[:, None, :]
    sine_part = jnp.concatenate([jnp.sin(angles), jnp.sin(angles)], axis=-1)[:, None, :]
    return (cosine, sine_part)


def rotate(field_in, cosine, sine_part):
    half_rot = ROT // 2
    first_half = field_in[..., :half_rot]
    second = field_in[..., half_rot:ROT]
    turned = jnp.concatenate([-second, first_half], axis=-1)
    return jnp.concatenate(
        [field_in[..., :ROT] * cosine + turned * sine_part, field_in[..., ROT:]], axis=-1
    )


def unrotate(grad_in, cosine, sine_part):
    half_rot = ROT // 2
    head_part = grad_in[..., :ROT]
    scaled = head_part * sine_part
    turned = jnp.concatenate([scaled[..., half_rot:], -scaled[..., :half_rot]], axis=-1)
    return jnp.concatenate([head_part * cosine + turned, grad_in[..., ROT:]], axis=-1)


def normalize(raw_rows):
    average = jnp.mean(raw_rows, axis=-1, keepdims=True)
    centred = raw_rows - average
    spread = jnp.mean(centred * centred, axis=-1, keepdims=True)
    inverse_root = lax.rsqrt(spread + epsilon)
    return (centred * inverse_root, inverse_root)


def against(left, right):
    return lax.dot_general(
        left, right, (((1,), (1,)), ((), ())), preferred_element_type=jnp.float32
    )


def per_device(
    tokens,
    cotangent,
    gain_attn,
    bias_attn,
    gain_mlp,
    bias_mlp,
    qkv_weight,
    qkv_bias,
    out_weight,
    out_bias,
    up_weight,
    up_bias,
    down_weight,
    down_bias,
):
    own_rows = tokens.shape[0]
    model_width = tokens.shape[1]
    heads_here = out_weight.shape[0] // HD
    score_scale = HD ** (-0.5)
    whole_rows = lax.all_gather(tokens, "tensor", axis=0, tiled=True)
    seq_len = whole_rows.shape[0]
    normed, _ = normalize(whole_rows.astype(jnp.float32))
    attention_input = (normed * gain_attn + bias_attn).astype(jnp.bfloat16)
    feed_input = (normed * gain_mlp + bias_mlp).astype(jnp.bfloat16)
    projected = jnp.dot(attention_input, qkv_weight, preferred_element_type=jnp.float32) + qkv_bias
    projected = projected.reshape(seq_len, heads_here, 3, HD)
    cosine, sine_part = angle_tables(seq_len)
    queries = rotate(projected[:, :, 0], cosine, sine_part).astype(jnp.bfloat16)
    keys_all = rotate(projected[:, :, 1], cosine, sine_part).astype(jnp.bfloat16)
    values_all = projected[:, :, 2].astype(jnp.bfloat16)
    preact = jnp.dot(feed_input, up_weight, preferred_element_type=jnp.float32) + up_bias
    hidden = jax.nn.gelu(preact, approximate=False).astype(jnp.bfloat16)
    block_rows = min(512, seq_len)
    block_total = seq_len // block_rows
    key_positions = jnp.arange(seq_len, dtype=jnp.int32)

    def causal_mask(offset):
        return key_positions[None, :] <= (offset + jnp.arange(block_rows, dtype=jnp.int32))[:, None]

    def forward_block(number):
        offset = number * block_rows
        query_rows = lax.dynamic_slice_in_dim(queries, offset, block_rows, 0)
        scores = (
            jnp.einsum("qhd,khd->hqk", query_rows, keys_all, preferred_element_type=jnp.float32)
            * score_scale
        )
        scores = jnp.where(causal_mask(offset)[None], scores, -1e30)
        highest = jnp.max(scores, axis=-1, keepdims=True)
        weights = jnp.exp(scores - highest)
        totals = jnp.sum(weights, axis=-1, keepdims=True)
        soft_rows = (weights / totals).astype(jnp.bfloat16)
        context_rows = jnp.einsum(
            "hqk,khd->qhd", soft_rows, values_all, preferred_element_type=jnp.float32
        ).astype(jnp.bfloat16)
        log_totals = (highest + jnp.log(totals))[:, :, 0].T
        return (context_rows, log_totals)

    context_blocks, log_blocks = lax.map(forward_block, jnp.arange(block_total, dtype=jnp.int32))
    context = context_blocks.reshape(seq_len, heads_here * HD)
    log_sums = log_blocks.reshape(seq_len, heads_here)
    context_rows = context
    branch = lax.psum_scatter(
        jnp.dot(context_rows, out_weight, preferred_element_type=jnp.float32)
        + jnp.dot(hidden, down_weight, preferred_element_type=jnp.float32),
        "tensor",
        scatter_dimension=0,
        tiled=True,
    )
    branch = branch + out_bias + down_bias
    residual_out = tokens.astype(jnp.float32) + branch
    mixed_out = residual_out.astype(jnp.bfloat16)
    forward_squares = jnp.stack([jnp.sum(residual_out * residual_out), jnp.sum(branch * branch)])
    forward_totals = lax.psum(forward_squares, ("dp", "tensor"))
    upstream = lax.all_gather(cotangent, "tensor", axis=0, tiled=True)
    out_weight_grad = jnp.einsum("sa,sd->ad", context, upstream, preferred_element_type=jnp.float32)
    down_weight_grad = jnp.einsum("sf,sd->fd", hidden, upstream, preferred_element_type=jnp.float32)
    context_grad = against(upstream, out_weight).astype(jnp.bfloat16)
    hidden_grad = against(upstream, down_weight)
    normal_cdf = 0.5 * (1.0 + lax.erf(preact * 0.5**0.5))
    density = jnp.exp(-0.5 * preact * preact) * (1.0 / math.sqrt(2.0 * math.pi))
    preact_grad = (hidden_grad * (normal_cdf + preact * density)).astype(jnp.bfloat16)
    context_grad3 = context_grad.reshape(seq_len, heads_here, HD)

    def backward_block(carried, number):
        key_grad, value_grad = carried
        offset = number * block_rows
        query_rows = lax.dynamic_slice_in_dim(queries, offset, block_rows, 0)
        grad_rows = lax.dynamic_slice_in_dim(context_grad3, offset, block_rows, 0)
        log_rows = lax.dynamic_slice_in_dim(log_sums, offset, block_rows, 0).T
        scores = (
            jnp.einsum("qhd,khd->hqk", query_rows, keys_all, preferred_element_type=jnp.float32)
            * score_scale
        )
        soft_full = jnp.exp(
            jnp.where(causal_mask(offset)[None], scores - log_rows[:, :, None], -1e30)
        )
        prob_grad = jnp.einsum(
            "qhd,khd->hqk", grad_rows, values_all, preferred_element_type=jnp.float32
        )
        deltas = jnp.sum(soft_full * prob_grad, axis=-1, keepdims=True)
        score_grad = (soft_full * (prob_grad - deltas)).astype(jnp.bfloat16)
        query_grad = (
            jnp.einsum("hqk,khd->qhd", score_grad, keys_all, preferred_element_type=jnp.float32)
            * score_scale
        )
        key_grad = (
            key_grad
            + jnp.einsum("hqk,qhd->khd", score_grad, query_rows, preferred_element_type=jnp.float32)
            * score_scale
        )
        value_grad = value_grad + jnp.einsum(
            "hqk,qhd->khd",
            soft_full.astype(jnp.bfloat16),
            grad_rows,
            preferred_element_type=jnp.float32,
        )
        return ((key_grad, value_grad), query_grad)

    empty = jnp.zeros((seq_len, heads_here, HD), jnp.float32)
    (key_grad, value_grad), query_blocks = lax.scan(
        backward_block, (empty, empty), jnp.arange(block_total, dtype=jnp.int32)
    )
    query_grad = unrotate(query_blocks.reshape(seq_len, heads_here, HD), cosine, sine_part)
    key_grad = unrotate(key_grad, cosine, sine_part)
    qkv_grad = (
        jnp.stack([query_grad, key_grad, value_grad], axis=2)
        .reshape(seq_len, 3 * heads_here * HD)
        .astype(jnp.bfloat16)
    )
    qkv_weight_grad = jnp.einsum(
        "sd,sc->dc", attention_input, qkv_grad, preferred_element_type=jnp.float32
    )
    qkv_bias_grad = jnp.sum(qkv_grad, axis=0, dtype=jnp.float32)
    up_weight_grad = jnp.einsum(
        "sd,sf->df", feed_input, preact_grad, preferred_element_type=jnp.float32
    )
    up_bias_grad = jnp.sum(preact_grad, axis=0, dtype=jnp.float32)
    own_normed, own_scale = normalize(tokens.astype(jnp.float32))
    attention_back = against(qkv_grad, qkv_weight)
    feed_back = against(preact_grad, up_weight)
    gain_terms = jnp.stack(
        [
            jnp.sum(normed * attention_back, axis=0),
            jnp.sum(attention_back, axis=0),
            jnp.sum(normed * feed_back, axis=0),
            jnp.sum(feed_back, axis=0),
        ]
    )
    normed_grad = lax.psum_scatter(
        (attention_back * gain_attn + feed_back * gain_mlp).astype(jnp.bfloat16),
        "tensor",
        scatter_dimension=0,
        tiled=True,
    ).astype(jnp.float32)
    centred_term = (
        normed_grad
        - jnp.mean(normed_grad, axis=-1, keepdims=True)
        - own_normed * jnp.mean(normed_grad * own_normed, axis=-1, keepdims=True)
    )
    input_grad = own_scale * centred_term + cotangent.astype(jnp.float32)
    (
        qkv_weight_grad,
        qkv_bias_grad,
        out_weight_grad,
        up_weight_grad,
        up_bias_grad,
        down_weight_grad,
    ) = lax.psum(
        (
            qkv_weight_grad,
            qkv_bias_grad,
            out_weight_grad,
            up_weight_grad,
            up_bias_grad,
            down_weight_grad,
        ),
        "dp",
    )
    bias_rows = jnp.sum(cotangent, axis=0, dtype=jnp.float32)
    grad_square = jnp.sum(input_grad * input_grad)
    gain_totals, bias_totals, grad_total = lax.psum(
        (gain_terms, bias_rows, grad_square), ("dp", "tensor")
    )
    square_totals = jnp.concatenate([forward_totals, grad_total[None]])
    elements = own_rows * model_width * lax.axis_size("dp") * lax.axis_size("tensor")
    statistics = jnp.sqrt(square_totals / elements)
    return (
        mixed_out,
        input_grad,
        gain_totals[0],
        gain_totals[1],
        gain_totals[2],
        gain_totals[3],
        qkv_weight_grad,
        qkv_bias_grad,
        out_weight_grad,
        bias_totals,
        up_weight_grad,
        up_bias_grad,
        down_weight_grad,
        bias_totals,
        statistics,
    )


def solution(mesh):
    in_specs = (
        P(("dp", "tensor"), None),
        P(("dp", "tensor"), None),
        P(),
        P(),
        P(),
        P(),
        P(None, "tensor"),
        P("tensor"),
        P("tensor", None),
        P(),
        P(None, "tensor"),
        P("tensor"),
        P("tensor", None),
        P(),
    )
    out_specs = (
        P(("dp", "tensor"), None),
        P(("dp", "tensor"), None),
        P(),
        P(),
        P(),
        P(),
        P(None, "tensor"),
        P("tensor"),
        P("tensor", None),
        P(),
        P(None, "tensor"),
        P("tensor"),
        P("tensor", None),
        P(),
        P(),
    )
    return jax.shard_map(
        per_device, mesh=mesh, in_specs=in_specs, out_specs=out_specs, check_vma=False
    )
```

profile of v0, /device:TPU:0, one launch (start us, length us, event | category | flops | bytes accessed | tf_op | source)
XLA Modules:
  0.0 678.1 jit_solution(6702302602257500573)
XLA Ops:
  9.1 25.9 %all-gather.3.cloned.1.call-done = bf16[1024,1024]{1,0:T(8,128)(2,1)} async-done(((bf16[256,1024]{1,0:T(8,128)(2,1)}), bf16[1024,1024]{1,0:T(8,128)(2,1)}) %all-gather.3.cloned.1.call-update) | async-done | bytes 2097168 | tf_op jit(solution)/shard_map/all_gather | solution.py:73
  44.1 21.8 %while.28 = (s32[]{:T(128)}, bf16[2,512,4,64]{1,3,2,0:T(8,128)(2,1)}, f32[2,512,4]{1,2,0:T(4,128)S(1)}, s32[2]{0:T(128)S(1)}, bf16[1024,4,64]{0,2,1:T(8,128)(2,1...) while((s32[]{:T(128)}, ...), condition=%wide.region_5.6_spmd.clone, body=%wide.region_2.5_spmd.clone.sunk | while | flops 562690560 | bytes 28906164 | solution.py:111
  50.7 4.3 fusion.150
  61.7 4.3 fusion.150
  69.1 72.1 %while.29 = (s32[]{:T(128)}, f32[1024,4,64]{0,2,1:T(8,128)}, f32[1024,4,64]{0,2,1:T(8,128)}, f32[2,512,4,64]{1,0,3,2:T(2,128)}, s32[2]{0:T(128)S(1)}, /*index=5*...) while((s32[]{:T(128)}, f32[1024,4,64]{0,2,1:T(8,128)}, ...), condition=%wide.region_11.12_spmd.clone, body=%wide.region_9.11_spmd.clone.sunk | while | flops 1375599104 | bytes 162591104 | solution.py:173
  73.5 4.7 multiply_reduce_fusion.5
  85.5 10.4 %dynamic_update_slice.22 = f32[2,512,4,64]{1,0,3,2:T(2,128)} dynamic-update-slice(f32[2,512,4,64]{1,0,3,2:T(2,128)} %get-tuple-element.430, f32[1,512,4,64]{1,0,3,2:T(1,128)} %copy.73, s32[]{:T(128)} %get-tuple-element.427, s32[]{:T(128)} %constant.73.clone.1..sunk.1, s32[]{:T(128)} %constant.73.clone.1..sunk.1, s32[]{:T(128)} %constant.73.clone.1..sunk.1) | dynamic-update-slice | bytes 1048580 | tf_op jit(solution)/shard_map/while/body/jit(dynamic_update_index_in_dim)/dynamic_update_slice | solution.py:173
  95.9 4.2 fusion.161
  108.7 4.7 multiply_reduce_fusion.5
  120.7 10.4 %dynamic_update_slice.22 = f32[2,512,4,64]{1,0,3,2:T(2,128)} dynamic-update-slice(f32[2,512,4,64]{1,0,3,2:T(2,128)} %get-tuple-element.430, f32[1,512,4,64]{1,0,3,2:T(1,128)} %copy.73, s32[]{:T(128)} %get-tuple-element.427, s32[]{:T(128)} %constant.73.clone.1..sunk.1, s32[]{:T(128)} %constant.73.clone.1..sunk.1, s32[]{:T(128)} %constant.73.clone.1..sunk.1) | dynamic-update-slice | bytes 1048580 | tf_op jit(solution)/shard_map/while/body/jit(dynamic_update_index_in_dim)/dynamic_update_slice | solution.py:173
  131.1 4.5 fusion.161
  136.5 4.7 fusion.162
  149.7 13.0 %fusion.55 = (bf16[1024,1024]{1,0:T(8,128)(2,1)}, f32[1024,1024]{1,0:T(8,128)S(1)}) fusion(f32[1024]{0:T(1024)S(1)} %copy-done.36, bf16[1024,1024]{1,0:T(8,128)(2,1)S(1)} %copy-done, bf16[1024,1024]{1,0:T(8,128)(2,1)S(1)} %copy-done.7, f32[1024]{0:T(1024)S(1)} %copy-done.41, f32[1024]{0:T(1024)S(1)} %copy-done.42, f32[1024]{0:T(1024)S(1)} %copy-done.30, ...), kind=kOutput, calls=%fused_computation.66 | convolution fusion | flops 2222981120 | bytes 10506240 | tf_op jit(solution)/shard_map/dot_general | solution.py:84
  162.7 3.9 convert_reduce_fusion.1
  169.1 4.4 fusion.50
  175.3 4.6 fusion.96
  186.3 6.1 fusion.89
  192.4 4.4 fusion.99
  196.8 4.8 fusion.85
  203.1 22.2 %all-reduce.1 = (f32[768]{0:T(1024)}, f32[1024]{0:T(1024)}) all-reduce(f32[768]{0:T(1024)S(1)} %reduce_sum.175, f32[1024]{0:T(1024)S(1)} %get-tuple-element.262), channel_id=1, replica_groups=mesh['dp'=8,'tensor'=4] {'dp'}, use_global_device_ids=true, to_apply=%region_22.23 | all-reduce | flops 1792 | bytes 14336 | tf_op jit(solution)/shard_map/psum | solution.py:221
  225.4 27.4 %reduce-scatter.3.cloned.1.call-done = f32[256,1024]{1,0:T(8,128)} async-done(((f32[1024,1024]{1,0:T(8,128)}), f32[256,1024]{1,0:T(8,128)}) %reduce-scatter.3.cloned.1.call-update) | async-done | bytes 1048592 | tf_op jit(solution)/shard_map/reduce_scatter | solution.py:115
  260.8 42.5 %all-reduce = (f32[4,1024]{1,0:T(4,128)S(1)}, f32[1024]{0:T(1024)S(1)}, f32[1]{0:T(128)}, f32[2]{0:T(128)S(1)}) all-reduce(f32[4,1024]{1,0:T(4,128)S(1)} %pad_maximum_fusion.4, f32[1024]{0:T(1024)S(1)} %get-tuple-element.243, f32[1]{0:T(128)} %bitcast.20, f32[2]{0:T(128)S(1)} %pad_maximum_fusion.5), channel_id=1, replica_groups=mesh['dp'=8,'tensor'=4] {'dp','tensor'}, use_global_device_ids=true, to_apply=%region_19.20 | all-reduce | flops 5123 | bytes 40984 | tf_op jit(solution)/shard_map/psum | solution.py:234
  305.2 355.0 %all-reduce.5.cloned.1.call-done = (f32[1024,768]{1,0:T(8,128)}, f32[256,1024]{1,0:T(8,128)}, f32[1024,1024]{1,0:T(8,128)}, f32[1024,1024]{1,0:T(8,128)}) async-done(((f32[1024,768]{1,0:T(8,128)}, f32[256,1024]{1,0:T(8,128)}, f32[1024,1024]{1,0:T(8,128)}, f32[1024,1024]{1,0:T(8,128)}), (f32[1024,768]{1,0:T(8,128)}, f32[256,1024]{1,0:T(8,128)}, f32[1024,1024]{1,0:T(8,128)}, ...) | async-done | bytes 12582928 | tf_op jit(solution)/shard_map/psum | solution.py:221
  660.8 3.9 copy.104
  (203 shorter events, 89.6 us)
Async XLA Ops:
  7.2 141.4 %copy-start = (bf16[1024,1024]{1,0:T(8,128)(2,1)S(1)}, bf16[1024,1024]{1,0:T(8,128)(2,1)}, u32[]{:S(2)}) copy-start(bf16[1024,1024]{1,0:T(8,128)(2,1)} %param.28) | copy-start | bytes 6291460
  7.2 32.1 %copy-start.37 = (f32[1024]{0:T(1024)S(1)}, f32[1024]{0:T(1024)}, u32[]{:S(2)}) copy-start(f32[1024]{0:T(1024)} %param.20) | copy-start | bytes 12292
  7.2 32.1 %copy-start.39 = (f32[1024]{0:T(1024)S(1)}, f32[1024]{0:T(1024)}, u32[]{:S(2)}) copy-start(f32[1024]{0:T(1024)} %param.21) | copy-start | bytes 12292
  7.2 32.1 %copy-start.35 = (f32[768]{0:T(1024)S(1)}, f32[768]{0:T(1024)}, u32[]{:S(2)}) copy-start(f32[768]{0:T(1024)} %param.25) | copy-start | bytes 9220
  7.2 27.7 %all-gather.3.cloned.1.call-start = ((), (), s32[]{:S(2)}) async-start(), calls=%async_computation.2 | async-start | bytes 2621440 | tf_op jit(solution)/shard_map/all_gather | solution.py:73
  8.0 58.0 %all-gather.5.cloned.1.call-start = ((), (), s32[]{:S(2)}) async-start(), calls=%async_computation.4 | async-start | bytes 2621440 | tf_op jit(solution)/shard_map/all_gather | solution.py:127
  8.7 216.7 %reduce-scatter.5.cloned.1.call-start = ((), (), s32[]{:S(2)}) async-start(), calls=%async_computation.5 | async-start | bytes 2621440 | tf_op jit(solution)/shard_map/reduce_scatter | solution.py:202
  9.0 34.1 %copy-start.19 = (f32[1024,16]{0,1:T(8,128)}, f32[1024,16]{0,1:T(8,128)S(1)}, u32[]{:S(2)}) copy-start(f32[1024,16]{0,1:T(8,128)S(1)} %get-tuple-element.267) | copy-start | bytes 196612
  9.1 34.1 %copy-start.21 = (f32[1024,16]{0,1:T(8,128)}, f32[1024,16]{0,1:T(8,128)S(1)}, u32[]{:S(2)}) copy-start(f32[1024,16]{0,1:T(8,128)S(1)} %get-tuple-element.266) | copy-start | bytes 196612
  44.1 21.8 %copy-start.23 = (bf16[256,1024]{1,0:T(8,128)(2,1)S(1)}, bf16[256,1024]{1,0:T(8,128)(2,1)}, u32[]{:S(2)}) copy-start(bf16[256,1024]{1,0:T(8,128)(2,1)} %param.26) | copy-start | bytes 1572868
  69.1 76.6 %copy-start.20 = (f32[1024,16]{0,1:T(8,128)S(1)}, f32[1024,16]{0,1:T(8,128)}, u32[]{:S(2)}) copy-start(f32[1024,16]{0,1:T(8,128)} %copy-done.19) | copy-start | bytes 196612
  141.2 5.6 copy-start.4
  141.2 5.7 copy-start.22
  149.6 19.4 %copy-start.16 = (bf16[1024,4,3,64]{0,3,2,1:T(8,128)(2,1)}, bf16[1024,4,3,64]{0,3,2,1:T(8,128)(2,1)S(1)}, u32[]{:S(2)}) copy-start(bf16[1024,4,3,64]{0,3,2,1:T(8,128)(2,1)S(1)} %copy.43) | copy-start | bytes 4718596
  149.6 13.1 %copy-start.13 = (bf16[1024,1024]{1,0:T(8,128)(2,1)S(1)}, bf16[1024,1024]{1,0:T(8,128)(2,1)}, u32[]{:S(2)}) copy-start(bf16[1024,1024]{1,0:T(8,128)(2,1)} %all-gather.5.cloned.1.call-done) | copy-start | bytes 6291460
  149.6 13.1 %copy-start.32 = (bf16[1024,1024]{1,0:T(8,128)(2,1)S(1)}, bf16[1024,1024]{1,0:T(8,128)(2,1)}, u32[]{:S(2)}) copy-start(bf16[1024,1024]{1,0:T(8,128)(2,1)} %param.30) | copy-start | bytes 6291460
  173.5 79.3 %reduce-scatter.3.cloned.1.call-start = ((), (), s32[]{:S(2)}) async-start(), calls=%async_computation.3 | async-start | bytes 5242880 | tf_op jit(solution)/shard_map/reduce_scatter | solution.py:115
  182.7 477.5 %all-reduce.5.cloned.1.call-start = ((), (), s32[]{:S(2)}) async-start(), calls=%async_computation.6 | async-start | bytes 25165824 | tf_op jit(solution)/shard_map/psum | solution.py:221
  186.3 6.1 copy-start.14
  186.3 6.1 copy-start.45
  201.6 51.3 %copy-start.27 = (f32[1024]{0:T(1024)S(1)}, f32[1024]{0:T(1024)}, u32[]{:S(2)}) copy-start(f32[1024]{0:T(1024)} %param.31) | copy-start | bytes 12292
  201.6 51.3 %copy-start.28 = (f32[1024]{0:T(1024)S(1)}, f32[1024]{0:T(1024)}, u32[]{:S(2)}) copy-start(f32[1024]{0:T(1024)} %param.27) | copy-start | bytes 12292
  201.6 56.1 %copy-start.15 = (bf16[256,1024]{1,0:T(8,128)(2,1)S(1)}, bf16[256,1024]{1,0:T(8,128)(2,1)}, u32[]{:S(2)}) copy-start(bf16[256,1024]{1,0:T(8,128)(2,1)} %param.19) | copy-start | bytes 1572868
  303.3 362.4 %copy-start.31 = (f32[1024]{0:T(1024)}, f32[1024]{0:T(1024)S(1)}, u32[]{:S(2)}) copy-start(f32[1024]{0:T(1024)S(1)} %get-tuple-element.494) | copy-start | bytes 12292
  (32 other events, 108.2 us)
Sparse Core Ops, SparseCore 0:
  9.6 25.2 all-gather.2
  36.5 22.5 all-gather.4
  173.7 31.4 reduce-scatter.4
  208.3 44.5 reduce-scatter.2
  258.6 401.5 all-reduce.4
where the time goes:
time: 687 us; the launch traced here: 678 us
  waiting for transfers between devices  410 us (60%)
  matrix products  103 us (15%)
  blocking collectives  64.8 us (9%)
  local copies, waits for them, and re-layouts  53.5 us (8%)
  other arithmetic  28.8 us (4%)
  between operations  14.6 us (2%)
    psum x1, waiting for transfers between devices, per_device(): lax.psum((qkv_weight_grad, qkv_bias_grad, out_weight_grad, up_weight_grad...  355 us
    psum x1, blocking collectives, per_device(): lax.psum((gain_terms, bias_rows, grad_square), ('dp', 'tensor'))  42.5 us
    reduce_scatter x1, waiting for transfers between devices, per_device(): lax.psum_scatter(jnp.dot(context_rows, out_weight, preferred_element_type...  27.4 us
    all_gather x1, waiting for transfers between devices, per_device(): whole_rows = lax.all_gather(tokens, 'tensor', axis=0, tiled=True)  25.9 us
    dynamic_update_slice x4, local copies, waits for them, and re-layouts, per_device(): lax.scan(backward_block, (empty, empty), jnp.arange(block_total, dtype=jn...  23.5 us
    psum x1, blocking collectives, per_device(): lax.psum((qkv_weight_grad, qkv_bias_grad, out_weight_grad, up_weight_grad...  22.2 us
    dot_general x4, matrix products, against(): lax.dot_general(left, right, (((1,), (1,)), ((), ())), preferred_element_...  13.9 us
  transfers between devices with their start and end apart: 5, of which 3 were waited for; matrix products, arithmetic and copies ran while one was open for 10% of the time, Pallas kernels for 0%

commit v1 on v0

--- a/solution.py
+++ b/solution.py
@@ -232,7 +232,7 @@
     bias_rows = jnp.sum(cotangent, axis=0, dtype=jnp.float32)
     grad_square = jnp.sum(input_grad * input_grad)
     gain_totals, bias_totals, grad_total = lax.psum(
-        (gain_terms, bias_rows, grad_square), ("dp", "tensor")
+        lax.psum((gain_terms, bias_rows, grad_square), "tensor"), "dp"
     )
     square_totals = jnp.concatenate([forward_totals, grad_total[None]])
     elements = own_rows * model_width * lax.axis_size("dp") * lax.axis_size("tensor")

time: 687 us -> 688 us (level)
  waiting for transfers between devices: 410 us -> 380 us
  blocking collectives: 64.8 us -> 94.6 us
    psum x1, waiting for transfers between devices: 355 us -> 303 us  [per_device(): lax.psum((qkv_weight_grad, qkv_bias_grad, out_weight_grad, up_weight_grad...]
    psum x2 -> x3, blocking collectives: 64.8 us -> 94.6 us  [the longest x1 42.3 us: per_device(): forward_totals = lax.psum(forward_squares, ('dp', 'tensor'))]
    reduce_scatter x1, waiting for transfers between devices: 27.4 us -> 47.6 us  [per_device(): lax.psum_scatter(jnp.dot(context_rows, out_weight, preferred_element_type...]
  transfers between devices with their start and end apart: 5 -> 5, of which waited for: 3 -> 4; matrix products, arithmetic and copies ran while one was open for 10% -> 10% of each run, Pallas kernels for 0% -> 0%
where the time goes in v1:
time: 688 us; the launch traced here: 679 us
  waiting for transfers between devices  380 us (55%)
  matrix products  103 us (15%)
  blocking collectives  94.6 us (14%)
  local copies, waits for them, and re-layouts  53.5 us (8%)
  other arithmetic  28.8 us (4%)
  between operations  14.6 us (2%)
    psum x1, waiting for transfers between devices, per_device(): lax.psum((qkv_weight_grad, qkv_bias_grad, out_weight_grad, up_weight_grad...  303 us
    reduce_scatter x1, waiting for transfers between devices, per_device(): lax.psum_scatter(jnp.dot(context_rows, out_weight, preferred_element_type...  47.6 us
    psum x1, blocking collectives, per_device(): forward_totals = lax.psum(forward_squares, ('dp', 'tensor'))  42.3 us
    psum x1, blocking collectives, per_device(): lax.psum(lax.psum((gain_terms, bias_rows, grad_square), 'tensor'), 'dp')  40.2 us
    all_gather x1, waiting for transfers between devices, per_device(): whole_rows = lax.all_gather(tokens, 'tensor', axis=0, tiled=True)  25.9 us
    dynamic_update_slice x4, local copies, waits for them, and re-layouts, per_device(): lax.scan(backward_block, (empty, empty), jnp.arange(block_total, dtype=jn...  23.5 us
    dot_general x4, matrix products, against(): lax.dot_general(left, right, (((1,), (1,)), ((), ())), preferred_element_...  13.9 us
  transfers between devices with their start and end apart: 5, of which 4 were waited for; matrix products, arithmetic and copies ran while one was open for 10% of the time, Pallas kernels for 0%

profile of v1, /device:TPU:0, one launch (start us, length us, event | category | flops | bytes accessed | tf_op | source)
XLA Modules:
  0.0 678.6 jit_solution(1260742629875260082)
XLA Ops:
  9.1 25.9 %all-gather.3.cloned.1.call-done = bf16[1024,1024]{1,0:T(8,128)(2,1)} async-done(((bf16[256,1024]{1,0:T(8,128)(2,1)}), bf16[1024,1024]{1,0:T(8,128)(2,1)}) %all-gather.3.cloned.1.call-update) | async-done | bytes 2097168 | tf_op jit(solution)/shard_map/all_gather | solution.py:73
  44.1 21.8 %while.28 = (s32[]{:T(128)}, bf16[2,512,4,64]{1,3,2,0:T(8,128)(2,1)}, f32[2,512,4]{1,2,0:T(4,128)S(1)}, s32[2]{0:T(128)S(1)}, bf16[1024,4,64]{0,2,1:T(8,128)(2,1...) while((s32[]{:T(128)}, ...), condition=%wide.region_5.6_spmd.clone, body=%wide.region_2.5_spmd.clone.sunk | while | flops 562690560 | bytes 28906164 | solution.py:111
  50.7 4.3 fusion.150
  61.6 4.3 fusion.150
  69.1 72.1 %while.29 = (s32[]{:T(128)}, f32[1024,4,64]{0,2,1:T(8,128)}, f32[1024,4,64]{0,2,1:T(8,128)}, f32[2,512,4,64]{1,0,3,2:T(2,128)}, s32[2]{0:T(128)S(1)}, /*index=5*...) while((s32[]{:T(128)}, f32[1024,4,64]{0,2,1:T(8,128)}, ...), condition=%wide.region_11.12_spmd.clone, body=%wide.region_9.11_spmd.clone.sunk | while | flops 1375599104 | bytes 162591104 | solution.py:173
  73.5 4.7 multiply_reduce_fusion.5
  85.5 10.4 %dynamic_update_slice.22 = f32[2,512,4,64]{1,0,3,2:T(2,128)} dynamic-update-slice(f32[2,512,4,64]{1,0,3,2:T(2,128)} %get-tuple-element.432, f32[1,512,4,64]{1,0,3,2:T(1,128)} %copy.73, s32[]{:T(128)} %get-tuple-element.429, s32[]{:T(128)} %constant.73.clone.1..sunk.1, s32[]{:T(128)} %constant.73.clone.1..sunk.1, s32[]{:T(128)} %constant.73.clone.1..sunk.1) | dynamic-update-slice | bytes 1048580 | tf_op jit(solution)/shard_map/while/body/jit(dynamic_update_index_in_dim)/dynamic_update_slice | solution.py:173
  95.9 4.2 fusion.161
  108.7 4.7 multiply_reduce_fusion.5
  120.6 10.4 %dynamic_update_slice.22 = f32[2,512,4,64]{1,0,3,2:T(2,128)} dynamic-update-slice(f32[2,512,4,64]{1,0,3,2:T(2,128)} %get-tuple-element.432, f32[1,512,4,64]{1,0,3,2:T(1,128)} %copy.73, s32[]{:T(128)} %get-tuple-element.429, s32[]{:T(128)} %constant.73.clone.1..sunk.1, s32[]{:T(128)} %constant.73.clone.1..sunk.1, s32[]{:T(128)} %constant.73.clone.1..sunk.1) | dynamic-update-slice | bytes 1048580 | tf_op jit(solution)/shard_map/while/body/jit(dynamic_update_index_in_dim)/dynamic_update_slice | solution.py:173
  131.1 4.5 fusion.161
  136.5 4.7 fusion.162
  149.6 13.0 %fusion.55 = (bf16[1024,1024]{1,0:T(8,128)(2,1)}, f32[1024,1024]{1,0:T(8,128)S(1)}) fusion(f32[1024]{0:T(1024)S(1)} %copy-done.36, bf16[1024,1024]{1,0:T(8,128)(2,1)S(1)} %copy-done, bf16[1024,1024]{1,0:T(8,128)(2,1)S(1)} %copy-done.7, f32[1024]{0:T(1024)S(1)} %copy-done.41, f32[1024]{0:T(1024)S(1)} %copy-done.42, f32[1024]{0:T(1024)S(1)} %copy-done.30, ...), kind=kOutput, calls=%fused_computation.66 | convolution fusion | flops 2222981120 | bytes 10506240 | tf_op jit(solution)/shard_map/dot_general | solution.py:84
  162.7 3.9 convert_reduce_fusion.1
  169.1 4.4 fusion.50
  175.3 4.6 fusion.96
  186.3 6.1 fusion.89
  192.4 4.4 fusion.99
  196.8 4.8 fusion.85
  205.2 47.6 %reduce-scatter.3.cloned.1.call-done = f32[256,1024]{1,0:T(8,128)} async-done(((f32[1024,1024]{1,0:T(8,128)}), f32[256,1024]{1,0:T(8,128)}) %reduce-scatter.3.cloned.1.call-update) | async-done | bytes 1048592 | tf_op jit(solution)/shard_map/reduce_scatter | solution.py:115
  257.7 42.3 %psum.101 = f32[2]{0:T(128)S(1)} all-reduce(f32[2]{0:T(128)S(1)} %pad_maximum_fusion.5), channel_id=1, replica_groups=mesh['dp'=8,'tensor'=4] {'dp','tensor'}, use_global_device_ids=true, to_apply=%region_34.35 | all-reduce | flops 2 | bytes 16 | tf_op jit(solution)/shard_map/psum | solution.py:126
  303.1 12.1 %all-reduce.2 = (f32[4,1024]{1,0:T(4,128)S(1)}, f32[1024]{0:T(1024)S(1)}, f32[]{:T(128)}) all-reduce(f32[4,1024]{1,0:T(4,128)S(1)} %pad_maximum_fusion.4, f32[1024]{0:T(1024)S(1)} %get-tuple-element.245, f32[]{:T(128)} %get-tuple-element.231), channel_id=1, replica_groups=mesh['dp'=8,'tensor'=4] {'tensor'}, use_global_device_ids=true, to_apply=%region_19.20 | all-reduce | flops 5121 | bytes 40968 | tf_op jit(solution)/shard_map/psum | solution.py:235
  315.2 40.2 %all-reduce = (f32[4,1024]{1,0:T(4,128)S(1)}, f32[768]{0:T(1024)}, f32[1024]{0:T(1024)S(1)}, f32[1024]{0:T(1024)}, f32[1]{0:T(128)}) all-reduce(f32[4,1024]{1,0:T(4,128)S(1)} %get-tuple-element.226, f32[768]{0:T(1024)S(1)} %reduce_sum.175, f32[1024]{0:T(1024)S(1)} %get-tuple-element.227, ...), channel_id=1, replica_groups=mesh['dp'=8,'tensor'=4] {'dp'}, use_global_device_ids=true, to_apply=%region_20.21 | all-reduce | flops 6913 | bytes 55304 | tf_op jit(solution)/shard_map/psum | solution.py:234
  357.3 303.4 %all-reduce.5.cloned.1.call-done = (f32[1024,768]{1,0:T(8,128)}, f32[256,1024]{1,0:T(8,128)}, f32[1024,1024]{1,0:T(8,128)}, f32[1024,1024]{1,0:T(8,128)}) async-done(((f32[1024,768]{1,0:T(8,128)}, f32[256,1024]{1,0:T(8,128)}, f32[1024,1024]{1,0:T(8,128)}, f32[1024,1024]{1,0:T(8,128)}), (f32[1024,768]{1,0:T(8,128)}, f32[256,1024]{1,0:T(8,128)}, f32[1024,1024]{1,0:T(8,128)}, ...) | async-done | bytes 12582928 | tf_op jit(solution)/shard_map/psum | solution.py:221
  (204 shorter events, 95.6 us)
Async XLA Ops:
  7.2 141.4 %copy-start = (bf16[1024,1024]{1,0:T(8,128)(2,1)S(1)}, bf16[1024,1024]{1,0:T(8,128)(2,1)}, u32[]{:S(2)}) copy-start(bf16[1024,1024]{1,0:T(8,128)(2,1)} %param.28) | copy-start | bytes 6291460
  7.2 32.1 %copy-start.37 = (f32[1024]{0:T(1024)S(1)}, f32[1024]{0:T(1024)}, u32[]{:S(2)}) copy-start(f32[1024]{0:T(1024)} %param.20) | copy-start | bytes 12292
  7.2 32.1 %copy-start.39 = (f32[1024]{0:T(1024)S(1)}, f32[1024]{0:T(1024)}, u32[]{:S(2)}) copy-start(f32[1024]{0:T(1024)} %param.21) | copy-start | bytes 12292
  7.2 32.1 %copy-start.35 = (f32[768]{0:T(1024)S(1)}, f32[768]{0:T(1024)}, u32[]{:S(2)}) copy-start(f32[768]{0:T(1024)} %param.25) | copy-start | bytes 9220
  7.2 27.7 %all-gather.3.cloned.1.call-start = ((), (), s32[]{:S(2)}) async-start(), calls=%async_computation.2 | async-start | bytes 2621440 | tf_op jit(solution)/shard_map/all_gather | solution.py:73
  8.0 58.0 %all-gather.5.cloned.1.call-start = ((), (), s32[]{:S(2)}) async-start(), calls=%async_computation.4 | async-start | bytes 2621440 | tf_op jit(solution)/shard_map/all_gather | solution.py:127
  8.7 196.4 %reduce-scatter.5.cloned.1.call-start = ((), (), s32[]{:S(2)}) async-start(), calls=%async_computation.5 | async-start | bytes 2621440 | tf_op jit(solution)/shard_map/reduce_scatter | solution.py:202
  9.0 34.1 %copy-start.19 = (f32[1024,16]{0,1:T(8,128)}, f32[1024,16]{0,1:T(8,128)S(1)}, u32[]{:S(2)}) copy-start(f32[1024,16]{0,1:T(8,128)S(1)} %get-tuple-element.269) | copy-start | bytes 196612
  9.1 34.1 %copy-start.21 = (f32[1024,16]{0,1:T(8,128)}, f32[1024,16]{0,1:T(8,128)S(1)}, u32[]{:S(2)}) copy-start(f32[1024,16]{0,1:T(8,128)S(1)} %get-tuple-element.268) | copy-start | bytes 196612
  44.1 21.8 %copy-start.23 = (bf16[256,1024]{1,0:T(8,128)(2,1)S(1)}, bf16[256,1024]{1,0:T(8,128)(2,1)}, u32[]{:S(2)}) copy-start(bf16[256,1024]{1,0:T(8,128)(2,1)} %param.26) | copy-start | bytes 1572868
  69.1 76.6 %copy-start.20 = (f32[1024,16]{0,1:T(8,128)S(1)}, f32[1024,16]{0,1:T(8,128)}, u32[]{:S(2)}) copy-start(f32[1024,16]{0,1:T(8,128)} %copy-done.19) | copy-start | bytes 196612
  141.2 5.6 copy-start.4
  141.2 5.7 copy-start.22
  149.6 19.4 %copy-start.16 = (bf16[1024,4,3,64]{0,3,2,1:T(8,128)(2,1)}, bf16[1024,4,3,64]{0,3,2,1:T(8,128)(2,1)S(1)}, u32[]{:S(2)}) copy-start(bf16[1024,4,3,64]{0,3,2,1:T(8,128)(2,1)S(1)} %copy.43) | copy-start | bytes 4718596
  149.6 13.1 %copy-start.13 = (bf16[1024,1024]{1,0:T(8,128)(2,1)S(1)}, bf16[1024,1024]{1,0:T(8,128)(2,1)}, u32[]{:S(2)}) copy-start(bf16[1024,1024]{1,0:T(8,128)(2,1)} %all-gather.5.cloned.1.call-done) | copy-start | bytes 6291460
  149.6 13.1 %copy-start.32 = (bf16[1024,1024]{1,0:T(8,128)(2,1)S(1)}, bf16[1024,1024]{1,0:T(8,128)(2,1)}, u32[]{:S(2)}) copy-start(bf16[1024,1024]{1,0:T(8,128)(2,1)} %param.30) | copy-start | bytes 6291460
  173.5 79.2 %reduce-scatter.3.cloned.1.call-start = ((), (), s32[]{:S(2)}) async-start(), calls=%async_computation.3 | async-start | bytes 5242880 | tf_op jit(solution)/shard_map/reduce_scatter | solution.py:115
  182.7 478.0 %all-reduce.5.cloned.1.call-start = ((), (), s32[]{:S(2)}) async-start(), calls=%async_computation.6 | async-start | bytes 25165824 | tf_op jit(solution)/shard_map/psum | solution.py:221
  186.3 6.1 copy-start.14
  186.3 6.1 copy-start.45
  201.6 51.2 %copy-start.27 = (f32[1024]{0:T(1024)S(1)}, f32[1024]{0:T(1024)}, u32[]{:S(2)}) copy-start(f32[1024]{0:T(1024)} %param.31) | copy-start | bytes 12292
  201.6 51.2 %copy-start.28 = (f32[1024]{0:T(1024)S(1)}, f32[1024]{0:T(1024)}, u32[]{:S(2)}) copy-start(f32[1024]{0:T(1024)} %param.27) | copy-start | bytes 12292
  201.6 98.4 %copy-start.15 = (bf16[256,1024]{1,0:T(8,128)(2,1)S(1)}, bf16[256,1024]{1,0:T(8,128)(2,1)}, u32[]{:S(2)}) copy-start(bf16[256,1024]{1,0:T(8,128)(2,1)} %param.19) | copy-start | bytes 1572868
  355.4 310.7 %copy-start.31 = (f32[1024]{0:T(1024)}, f32[1024]{0:T(1024)S(1)}, u32[]{:S(2)}) copy-start(f32[1024]{0:T(1024)S(1)} %get-tuple-element.496) | copy-start | bytes 12292
  (32 other events, 108.2 us)
Sparse Core Ops, SparseCore 0:
  9.6 25.2 all-gather.2
  36.5 22.5 all-gather.4
  173.7 31.4 reduce-scatter.4
  208.3 44.4 reduce-scatter.2
  258.5 402.0 all-reduce.4
